TPU v7x, 32 devices: a whole 2x2x4 slice. The times are simulated.
32 devices in a mesh: ia: 4 (over z), ja: 4 (over y, x), ka: 2 (over core).
Axes of the slice: x: 2, y: 2, z: 4, core: 2. Of those that a mesh axis runs over, the one named last changes fastest.
Arguments:
- blocks: bfloat16 [4, 4, 4, 128, 128, 128], P('ia', 'ja', 'ka'), may hold values from -6 to 6
- coordinates: int32 [3, 4, 4, 4], P(None, 'ia', 'ja', 'ka'), may hold values from 0 to 3, as said below
- occupancy: int32 [4, 4, 4], P('ia', 'ja', 'ka'), may hold values from 0 to 1, as said below
- second_factor: bfloat16 [4, 512, 1024], P('ja', ('ia', 'ka')), may hold values from -12 to 12
- third_factor: bfloat16 [2, 512, 1024], P('ka', ('ia', 'ja')), may hold values from -0.0234375 to 0.0234375
- inverse_first: bfloat16 [1024, 1024], replicated
- inverse_second: bfloat16 [1024, 1024], replicated
Outputs:
- first_new: bfloat16 [4, 512, 1024], P('ia', ('ja', 'ka'))
- second_new: bfloat16 [4, 512, 1024], P('ja', ('ia', 'ka'))
Inputs may be any that keep to these rules, and one draw needn't show every extreme that they name: `occupancy`: each device has two slots; its second slot is occupied only where its first is. A device with two blocks is followed along ka, cyclically, by a device with none. Some device holds two blocks. coordinates[0], [1], [2] of a slot are a block row among 4, a block row among 4 and a block layer among 4 of its device's ranges; the two slots of a device name different layers.
All inputs are finite; a program needn't handle non-finite values.
Results may differ from a plain program's by a relative error of at most 0.006.
Values may be sent and summed in bfloat16 or wider, within the bound.
A program may use at most 128 MiB of HBM per device.

v0:
```python
import jax
import jax.numpy as jnp
from jax import lax
from jax.sharding import PartitionSpec as P

IB = 4
JB = 4


def passed_along(block, axis, distance):
    devices = range(lax.axis_size(axis))
    route = [((i - distance) % len(devices), i) for i in devices]
    return lax.ppermute(block, axis, route)


def block_products(tensor_block, left_rows, layer_slab, contract):
    block_edge = tensor_block.shape[0]
    step_rows = max(block_edge // 4, 1)
    summed = jnp.zeros((block_edge, left_rows.shape[1]), jnp.float32)
    for first_row in range(0, block_edge, step_rows):
        khatri = left_rows[first_row : first_row + step_rows][:, None, :] * layer_slab[None, :, :]
        if contract == 1:
            block_part = tensor_block[:, first_row : first_row + step_rows, :]
            contraction = (((1, 2), (0, 1)), ((), ()))
        else:
            block_part = tensor_block[first_row : first_row + step_rows]
            contraction = (((0, 2), (0, 1)), ((), ()))
        summed = summed + lax.dot_general(
            block_part, khatri, contraction, preferred_element_type=jnp.float32
        )
    return summed


def place_rows(partial_value, addend, block_index):
    block_edge = addend.shape[0]
    row_start = block_index * block_edge
    current = lax.dynamic_slice_in_dim(partial_value, row_start, block_edge, 0)
    return lax.dynamic_update_slice_in_dim(partial_value, addend, row_start, 0)


def pick_rows(source, block_index, block_edge):
    return lax.dynamic_slice_in_dim(source, block_index * block_edge, block_edge, 0)


def body(
    blocks, coordinates, occupancy, second_factor, third_factor, inverse_first, inverse_second
):
    block_edge = blocks.shape[-1]
    rank_width = inverse_first.shape[0]
    own_blocks = blocks.reshape(2, block_edge, block_edge, block_edge)
    places = coordinates.reshape(3, 2)
    occupied = occupancy.reshape(2)
    second_rows = lax.all_gather(second_factor, ("ia", "ka"), axis=1, tiled=True)[0]
    layer_rows = lax.all_gather(third_factor, ("ia", "ja"), axis=1, tiled=True)[0]
    slot_meta = jnp.stack([occupied[1], places[0, 1], places[1, 1]]).astype(jnp.bfloat16)
    arrived, arrived_layer, arrived_meta = passed_along(
        (own_blocks[1], pick_rows(layer_rows, places[2, 1], block_edge), slot_meta), "ka", 1
    )
    arrived_index = arrived_meta.astype(jnp.int32)
    keep_own = occupied[0] > 0
    tensor_block = jnp.where(keep_own, own_blocks[0], arrived)
    layer_slab = jnp.where(keep_own, pick_rows(layer_rows, places[2, 0], block_edge), arrived_layer)
    row_block = jnp.where(keep_own, places[0, 0], arrived_index[1])
    col_block = jnp.where(keep_own, places[1, 0], arrived_index[2])
    weight = jnp.where(keep_own, 1, arrived_index[0]).astype(jnp.float32)
    first_partial = jnp.zeros((IB * block_edge, rank_width), jnp.float32)
    contribution = block_products(
        tensor_block, pick_rows(second_rows, col_block, block_edge), layer_slab, 1
    )
    first_partial = place_rows(first_partial, contribution * weight, row_block)
    summed_rows = lax.psum(first_partial, ("ja", "ka"))
    first_rows = jnp.dot(
        summed_rows.astype(jnp.bfloat16), inverse_first, preferred_element_type=jnp.float32
    ).astype(jnp.bfloat16)
    share_rows = first_rows.shape[0] // lax.axis_size(("ja", "ka"))
    first_new = lax.dynamic_slice_in_dim(
        first_rows, lax.axis_index(("ja", "ka")) * share_rows, share_rows, 0
    )
    second_partial = jnp.zeros((JB * block_edge, rank_width), jnp.float32)
    contribution = block_products(
        tensor_block, pick_rows(first_rows, row_block, block_edge), layer_slab, 0
    )
    second_partial = place_rows(second_partial, contribution * weight, col_block)
    owned_second = lax.psum_scatter(
        second_partial[None], ("ia", "ka"), scatter_dimension=1, tiled=True
    )[0]
    second_new = jnp.dot(
        owned_second.astype(jnp.bfloat16), inverse_second, preferred_element_type=jnp.float32
    ).astype(jnp.bfloat16)
    return (first_new[None], second_new[None])


def solution(mesh):
    in_specs = (
        P("ia", "ja", "ka", None, None, None),
        P(None, "ia", "ja", "ka"),
        P("ia", "ja", "ka"),
        P("ja", ("ia", "ka"), None),
        P("ka", ("ia", "ja"), None),
        P(),
        P(),
    )
    out_specs = (P("ia", ("ja", "ka"), None), P("ja", ("ia", "ka"), None))
    return jax.shard_map(body, mesh=mesh, in_specs=in_specs, out_specs=out_specs, check_vma=False)
```

profile of v0, /device:TPU:0, one launch (start us, length us, event | category | flops | bytes accessed | tf_op | source)
XLA Modules:
  0.0 221.0 jit_solution(3574953310530504106)
XLA Ops:
  7.2 0.0 copy-start
  7.2 0.0 copy-start.5
  7.2 0.0 copy-start.4
  7.2 0.0 all-gather.5.cloned.1.call-start
  7.2 4.9 %slice_bitcast_fusion = bf16[128,128,128]{2,1,0:T(8,128)(2,1)} fusion(bf16[1,1,2,128,128,128]{5,4,3,2,1,0:T(8,128)(2,1)} %param.7), kind=kLoop, calls=%fused_computation.33 | loop fusion | bytes 8388608 | tf_op jit(solution)/shard_map/squeeze | solution.py:57
  12.1 0.5 collective-permute-start
  12.6 0.0 all-gather.5.cloned.1.call-update
  12.6 0.0 all-gather.3.cloned.1.call-start
  12.7 0.7 all-gather.3.cloned.1.call-update
  13.4 0.0 reduce-scatter.2.cloned.1.call-start
  13.4 0.0 copy-done.5
  13.5 0.6 slice.105
  14.1 0.0 copy-done.4
  14.1 0.6 fusion.98
  15.4 0.7 fusion.100
  16.0 54.2 %all-gather.5.cloned.1.call-done = bf16[1,512,1024]{2,1,0:T(8,128)(2,1)} async-done(((bf16[1,32,1024]{2,1,0:T(8,128)(2,1)}), bf16[1,512,1024]{2,1,0:T(8,128)(2,1)}) %all-gather.5.cloned.1.call-update) | async-done | bytes 1048592 | tf_op jit(solution)/shard_map/all_gather | solution.py:54
  70.3 1.0 dynamic-slice_bitcast_fusion
  71.2 0.1 collective-permute-start.2
  71.3 2.0 pad_maximum_fusion
  73.4 0.5 collective-permute-start.1
  74.5 0.1 collective-permute-done.1
  74.7 0.7 fusion.99
  78.5 14.5 %all-gather.3.cloned.1.call-done = bf16[1,512,1024]{2,1,0:T(8,128)(2,1)} async-done(((bf16[1,64,1024]{2,1,0:T(8,128)(2,1)}), bf16[1,512,1024]{2,1,0:T(8,128)(2,1)}) %all-gather.3.cloned.1.call-update) | async-done | bytes 1048592 | tf_op jit(solution)/shard_map/all_gather | solution.py:53
  93.0 1.0 dynamic-slice_bitcast_fusion.5
  93.9 0.0 collective-permute-done.2
  93.9 1.0 bitcast_select_fusion.1
  95.0 0.0 collective-permute-done
  95.0 3.9 %bitcast_select_fusion = bf16[128,128,128]{2,1,0:T(8,128)(2,1)S(1)} fusion(bf16[128,128,128]{2,1,0:T(8,128)(2,1)} %collective-permute-done, bf16[1,1,2,128,128,128]{5,4,3,2,1,0:T(8,128)(2,1)} %param.7, pred[]{:T(512)} %bitcast), kind=kLoop, calls=%fused_computation.16 | loop fusion | flops 2097152 | bytes 12582913 | tf_op jit(solution)/shard_map/jit(_where)/select_n | solution.py:61
  98.9 0.8 fusion.97
  99.7 1.3 fusion.47
  101.0 1.3 fusion.50
  102.3 1.3 fusion.53
  103.7 1.6 broadcast.9
  105.3 2.1 fusion.86
  107.4 57.5 %all-reduce.1 = bf16[512,1024]{1,0:T(8,128)(2,1)S(1)} all-reduce(f32[512,1024]{1,0:T(8,128)} %fusion.86), channel_id=1, replica_groups=mesh['ia'=4,'ja'=4,'ka'=2] {'ja','ka'}, use_global_device_ids=true, to_apply=%region_0.1 | all-reduce | flops 524288 | bytes 3145728 | tf_op jit(solution)/shard_map/psum | solution.py:71
  164.9 0.0 copy-done
  164.9 1.3 convolution_convert_fusion
  166.2 0.0 copy-start.3
  166.2 1.0 copy-done.3
  167.2 2.6 %fusion.35 = f32[128,1024]{1,0:T(8,128)S(1)} fusion(bf16[128,128,128]{2,1,0:T(8,128)(2,1)} %copy-done.1, bf16[32,1024]{1,0:T(8,128)(2,1)S(1)} %get-tuple-element.8, bf16[128,1024]{1,0:T(8,128)(2,1)S(1)} %bitcast_select_fusion.1), kind=kOutput, calls=%fused_computation.36 | convolution fusion | flops 1090519040 | bytes 5046272 | tf_op jit(solution)/shard_map/dot_general | solution.py:28
  169.8 1.3 fusion.38
  171.2 1.3 fusion.41
  172.5 1.6 broadcast_in_dim.9
  174.1 2.3 %fusion.77 = f32[1,512,1024]{2,1,0:T(8,128)} fusion(f32[1,512,1024]{2,1,0:T(8,128)} %broadcast_in_dim.9, s32[]{:T(128)S(6)} %select_n.47, f32[128,1024]{1,0:T(8,128)S(1)} %fusion.41, f32[128,1024]{1,0:T(8,128)S(1)} %fusion.38, f32[128,1024]{1,0:T(8,128)S(1)} %fusion.35, bf16[128,128,128]{2,1,0:T(8,128)(2,1)S(1)} %copy-done.2, ...), kind=kOutput, calls=%fused_computation.50 | convolution fusion | flops 1091043328 | bytes 6619144 | tf_op jit(solution)/shard_map/dot_general | solution.py:28
  176.4 0.0 reduce-scatter.2.cloned.1.call-update
  176.5 1.6 dynamic-slice_bitcast_fusion.1
  178.0 33.6 %reduce-scatter.2.cloned.1.call-done = f32[1,64,1024]{2,1,0:T(8,128)} async-done(((f32[1,512,1024]{2,1,0:T(8,128)}), f32[1,64,1024]{2,1,0:T(8,128)}) %reduce-scatter.2.cloned.1.call-update) | async-done | bytes 262160 | tf_op jit(solution)/shard_map/reduce_scatter | solution.py:84
  211.6 2.8 %fusion.89 = bf16[1,64,1024]{2,1,0:T(8,128)(2,1)} fusion(bf16[1024,1024]{1,0:T(8,128)(2,1)} %param.13, f32[1,64,1024]{2,1,0:T(8,128)} %reduce-scatter.2.cloned.1.call-done), kind=kOutput, calls=%fused_computation.55 | convolution fusion | flops 134348800 | bytes 2490368 | tf_op jit(solution)/shard_map/dot_general | solution.py:87
  (8 shorter events, 0.0 us)
Async XLA Ops:
  7.2 157.8 %copy-start = (bf16[1024,1024]{1,0:T(8,128)(2,1)S(1)}, bf16[1024,1024]{1,0:T(8,128)(2,1)}, u32[]{:S(2)}) copy-start(bf16[1024,1024]{1,0:T(8,128)(2,1)} %param.12) | copy-start | bytes 6291460
  7.2 6.3 %copy-start.5 = (s32[1,1,2]{2,1,0:T(1,128)S(1)}, s32[1,1,2]{2,1,0:T(1,128)}, u32[]{:S(2)}) copy-start(s32[1,1,2]{2,1,0:T(1,128)} %param.9) | copy-start | bytes 28
  7.2 6.9 %copy-start.4 = (s32[3,1,1,2]{0,3,2,1:T(2,128)S(1)}, s32[3,1,1,2]{0,3,2,1:T(2,128)}, u32[]{:S(2)}) copy-start(s32[3,1,1,2]{0,3,2,1:T(2,128)} %param.8) | copy-start | bytes 76
  7.2 63.1 %all-gather.5.cloned.1.call-start = ((), (), s32[]{:S(2)}) async-start(), calls=%async_computation.2 | async-start | bytes 1114112 | tf_op jit(solution)/shard_map/all_gather | solution.py:54
  12.1 82.9 %collective-permute-start = (bf16[128,128,128]{2,1,0:T(8,128)(2,1)}, bf16[128,128,128]{2,1,0:T(8,128)(2,1)}, u32[]{:S(2)}, u32[]{:S(2)}) collective-permute-start(bf16[128,128,128]{2,1,0:T(8,128)(2,1)} %slice_bitcast_fusion), channel_id=1, source_target_pairs={{1,0},{0,1},{3,2},{2,3},{5,4},{4,5},{7,6},{6,7},{9,8},{8,9},{11,10... | collective-permute-start | bytes 12582920 | tf_op jit(solution)/shard_map/ppermute | solution.py:13
  12.6 80.3 %all-gather.3.cloned.1.call-start = ((), (), s32[]{:S(2)}) async-start(), calls=%async_computation.1 | async-start | bytes 1179648 | tf_op jit(solution)/shard_map/all_gather | solution.py:53
  13.4 198.3 %reduce-scatter.2.cloned.1.call-start = ((), (), s32[]{:S(2)}) async-start(), calls=%async_computation.3 | async-start | bytes 2359296 | tf_op jit(solution)/shard_map/reduce_scatter | solution.py:84
  71.2 22.7 %collective-permute-start.2 = (bf16[128,1024]{1,0:T(8,128)(2,1)S(1)}, bf16[128,1024]{1,0:T(8,128)(2,1)S(1)}, u32[]{:S(2)}, u32[]{:S(2)}) collective-permute-start(bf16[128,1024]{1,0:T(8,128)(2,1)S(1)} %dynamic-slice_bitcast_fusion), channel_id=1, source_target_pairs={{1,0},{0,1},{3,2},{2,3},{5,4},{4,5},{7,6},{6,7},{9,8},{8,9},{11,10... | collective-permute-start | bytes 786440 | tf_op jit(solution)/shard_map/ppermute | solution.py:13
  73.4 1.3 collective-permute-start.1
  98.9 2.1 copy-start.1
  166.2 1.0 copy-start.3
  167.2 2.7 %copy-start.2 = (bf16[128,128,128]{2,1,0:T(8,128)(2,1)S(1)}, bf16[128,128,128]{2,1,0:T(8,128)(2,1)}, u32[]{:S(2)}) copy-start(bf16[128,128,128]{2,1,0:T(8,128)(2,1)} %copy-done.1) | copy-start | bytes 12582916
Sparse Core Ops, SparseCore 0:
  12.8 57.4 all-gather.4
  71.9 21.0 all-gather.2
  176.6 35.0 reduce-scatter.1
where the time goes:
time: 221 us
  waiting for transfers between devices  103 us (47%)
  blocking collectives  57.5 us (26%)
  between operations  18.5 us (8%)
  matrix products  17.8 us (8%)
  local copies, waits for them, and re-layouts  16 us (7%)
  other arithmetic  6.99 us (3%)
    psum x1, blocking collectives, body(): summed_rows = lax.psum(first_partial, ('ja', 'ka'))  57.5 us
    all_gather x1, waiting for transfers between devices, body(): lax.all_gather(third_factor, ('ia', 'ja'), axis=1, tiled=True)[0]  54.2 us
    reduce_scatter x1, waiting for transfers between devices, body(): lax.psum_scatter(second_partial[None], ('ia', 'ka'), scatter_dimension=1,...  33.6 us
    all_gather x1, waiting for transfers between devices, body(): lax.all_gather(second_factor, ('ia', 'ka'), axis=1, tiled=True)[0]  14.5 us
    dot_general x8, matrix products, block_products(): lax.dot_general(block_part, khatri, contraction, preferred_element_type=j...  13.7 us
    squeeze x1, local copies, waits for them, and re-layouts, body(): own_blocks[1]  4.87 us
  transfers between devices with their start and end apart: 6, of which 4 were waited for; matrix products, arithmetic and copies ran while one was open for 4% of the time, Pallas kernels for 0%

commit v1 on v0

--- a/solution.py
+++ b/solution.py
@@ -5,6 +5,27 @@
 
 IB = 4
 JB = 4
+
+
+def collect(x, axis, dim):
+    peers, index, rows = (lax.axis_size(axis), lax.axis_index(axis), x.shape[dim])
+    right = [(i, (i + 1) % peers) for i in range(peers)]
+    downward = [(i, (i - 1) % peers) for i in range(peers)]
+    out = jnp.zeros((*x.shape[:dim], peers * rows, *x.shape[dim + 1 :]), x.dtype)
+    out = lax.dynamic_update_slice_in_dim(out, x, index * rows, axis=dim)
+    from_left = from_right = x
+    half = peers // 2
+    for turn in range(1, half + 1):
+        from_left = lax.ppermute(from_left, axis, right)
+        out = lax.dynamic_update_slice_in_dim(
+            out, from_left, (index - turn) % peers * rows, axis=dim
+        )
+        if turn < peers - half:
+            from_right = lax.ppermute(from_right, axis, downward)
+            out = lax.dynamic_update_slice_in_dim(
+                out, from_right, (index + turn) % peers * rows, axis=dim
+            )
+    return out
 
 
 def passed_along(block, axis, distance):
@@ -50,7 +71,7 @@
     own_blocks = blocks.reshape(2, block_edge, block_edge, block_edge)
     places = coordinates.reshape(3, 2)
     occupied = occupancy.reshape(2)
-    second_rows = lax.all_gather(second_factor, ("ia", "ka"), axis=1, tiled=True)[0]
+    second_rows = collect(second_factor, ("ia", "ka"), 1)[0]
     layer_rows = lax.all_gather(third_factor, ("ia", "ja"), axis=1, tiled=True)[0]
     slot_meta = jnp.stack([occupied[1], places[0, 1], places[1, 1]]).astype(jnp.bfloat16)
     arrived, arrived_layer, arrived_meta = passed_along(

time: 221 us -> 202 us (0.914)
  waiting for transfers between devices: 103 us -> 71.9 us
  starting transfers between devices: 1.18 us -> 12.5 us
    all_gather x1, waiting for transfers between devices: 54.2 us -> 31.1 us  [body(): lax.all_gather(third_factor, ('ia', 'ja'), axis=1, tiled=True)[0]]
    all_gather x1 -> x0, waiting for transfers between devices: 14.5 us -> none  [body(): lax.all_gather(second_factor, ('ia', 'ka'), axis=1, tiled=True)[0]]
    ppermute x0 -> x7, starting transfers between devices: none -> 11.8 us  [the longest x3 11.3 us: collect(): from_right = lax.ppermute(from_right, axis, downward)]
    ppermute x0 -> x7, waiting for transfers between devices: none -> 7.02 us  [the longest x4 7.01 us: collect(): from_left = lax.ppermute(from_left, axis, right)]
  transfers between devices with their start and end apart: 6 -> 12, of which waited for: 4 -> 5; matrix products, arithmetic and copies ran while one was open for 4% -> 4% of each run, Pallas kernels for 0% -> 0%
where the time goes in v1:
time: 202 us; the launch traced here: 201 us
  waiting for transfers between devices  71.9 us (36%)
  blocking collectives  58 us (29%)
  between operations  18.9 us (9%)
  matrix products  17.8 us (9%)
  local copies, waits for them, and re-layouts  15.1 us (7%)
  starting transfers between devices  12.5 us (6%)
  other arithmetic  6.89 us (3%)
    psum x1, blocking collectives, body(): summed_rows = lax.psum(first_partial, ('ja', 'ka'))  58 us
    reduce_scatter x1, waiting for transfers between devices, body(): lax.psum_scatter(second_partial[None], ('ia', 'ka'), scatter_dimension=1,...  32.4 us
    all_gather x1, waiting for transfers between devices, body(): lax.all_gather(third_factor, ('ia', 'ja'), axis=1, tiled=True)[0]  31.1 us
    dot_general x8, matrix products, block_products(): lax.dot_general(block_part, khatri, contraction, preferred_element_type=j...  13.7 us
    ppermute x3, starting transfers between devices, collect(): from_right = lax.ppermute(from_right, axis, downward)  11.3 us
    ppermute x4, waiting for transfers between devices, collect(): from_left = lax.ppermute(from_left, axis, right)  7.01 us
    squeeze x1, local copies, waits for them, and re-layouts, body(): own_blocks[1]  4.85 us
  transfers between devices with their start and end apart: 12, of which 5 were waited for; matrix products, arithmetic and copies ran while one was open for 4% of the time, Pallas kernels for 0%

profile of v1, /device:TPU:0, one launch (start us, length us, event | category | flops | bytes accessed | tf_op | source)
XLA Modules:
  0.0 201.2 jit_solution(318100358102554711)
XLA Ops:
  7.2 0.0 copy-start
  7.2 0.0 all-gather.2.cloned.1.call-start
  7.3 4.9 %slice_bitcast_fusion = bf16[128,128,128]{2,1,0:T(8,128)(2,1)} fusion(bf16[1,1,2,128,128,128]{5,4,3,2,1,0:T(8,128)(2,1)} %param.7), kind=kLoop, calls=%fused_computation.33 | loop fusion | bytes 8388608 | tf_op jit(solution)/shard_map/squeeze | solution.py:78
  12.1 0.5 collective-permute-start
  12.6 0.0 collective-permute-start.1
  12.6 4.7 %collective-permute-start.2 = (bf16[1,64,1024]{2,1,0:T(8,128)(2,1)S(1)}, bf16[1,64,1024]{2,1,0:T(8,128)(2,1)S(1)}, u32[]{:S(2)}, u32[]{:S(2)}) collective-permute-start(bf16[1,64,1024]{2,1,0:T(8,128)(2,1)S(1)} %copy-done.4), channel_id=1, source_target_pairs={{0,25},{1,0},{8,1},{9,8},{16,9},{17,16},{24,17},{25,24},{2,27},{3,... | collective-permute-start | bytes 393224 | tf_op jit(solution)/shard_map/ppermute | solution.py:24
  17.3 0.0 all-gather.2.cloned.1.call-update
  17.3 0.0 reduce-scatter.2.cloned.1.call-start
  17.4 0.6 fusion.100
  18.0 0.6 slice.101
  18.6 1.9 pad_maximum_fusion
  20.5 0.0 collective-permute-start.8
  20.6 0.1 squeeze.47
  20.7 0.6 fusion.98
  22.7 0.0 collective-permute-done.8
  22.7 0.7 fusion.99
  26.6 0.0 collective-permute-done.1
  26.6 0.5 collective-permute-start.3
  27.1 0.0 collective-permute-done.2
  27.1 3.1 %collective-permute-start.4 = (bf16[1,64,1024]{2,1,0:T(8,128)(2,1)S(1)}, bf16[1,64,1024]{2,1,0:T(8,128)(2,1)S(1)}, u32[]{:S(2)}, u32[]{:S(2)}) collective-permute-start(bf16[1,64,1024]{2,1,0:T(8,128)(2,1)S(1)} %collective-permute-done.2), channel_id=1, source_target_pairs={{0,25},{1,0},{8,1},{9,8},{16,9},{17,16},{24,17},{25,24},{2,27},{3,... | collective-permute-start | bytes 393224 | tf_op jit(solution)/shard_map/ppermute | solution.py:24
  30.2 3.8 %collective-permute-done.3 = bf16[1,64,1024]{2,1,0:T(8,128)(2,1)S(1)} collective-permute-done((bf16[1,64,1024]{2,1,0:T(8,128)(2,1)S(1)}, bf16[1,64,1024]{2,1,0:T(8,128)(2,1)S(1)}, u32[]{:S(2)}, u32[]{:S(2)}) %collective-permute-start.3) | collective-permute-done | bytes 131104 | tf_op jit(solution)/shard_map/ppermute | solution.py:19
  34.0 3.5 %collective-permute-start.6 = (bf16[1,64,1024]{2,1,0:T(8,128)(2,1)S(1)}, bf16[1,64,1024]{2,1,0:T(8,128)(2,1)S(1)}, u32[]{:S(2)}, u32[]{:S(2)}) collective-permute-start(bf16[1,64,1024]{2,1,0:T(8,128)(2,1)S(1)} %collective-permute-done.4), channel_id=1, source_target_pairs={{0,25},{1,0},{8,1},{9,8},{16,9},{17,16},{24,17},{25,24},{2,27},{3,... | collective-permute-start | bytes 393224 | tf_op jit(solution)/shard_map/ppermute | solution.py:24
  37.6 3.2 %collective-permute-done.5 = bf16[1,64,1024]{2,1,0:T(8,128)(2,1)S(1)} collective-permute-done((bf16[1,64,1024]{2,1,0:T(8,128)(2,1)S(1)}, bf16[1,64,1024]{2,1,0:T(8,128)(2,1)S(1)}, u32[]{:S(2)}, u32[]{:S(2)}) %collective-permute-start.5) | collective-permute-done | bytes 131104 | tf_op jit(solution)/shard_map/ppermute | solution.py:19
  40.8 0.0 collective-permute-start.7
  40.9 31.1 %all-gather.2.cloned.1.call-done = bf16[1,512,1024]{2,1,0:T(8,128)(2,1)} async-done(((bf16[1,32,1024]{2,1,0:T(8,128)(2,1)}), bf16[1,512,1024]{2,1,0:T(8,128)(2,1)}) %all-gather.2.cloned.1.call-update) | async-done | bytes 1048592 | tf_op jit(solution)/shard_map/all_gather | solution.py:75
  71.9 1.0 dynamic-slice_bitcast_fusion
  72.9 0.1 collective-permute-start.9
  73.1 1.4 collective-permute-done.9
  74.5 1.0 bitcast_select_fusion.1
  75.5 3.9 %bitcast_select_fusion = bf16[128,128,128]{2,1,0:T(8,128)(2,1)S(1)} fusion(bf16[128,128,128]{2,1,0:T(8,128)(2,1)} %collective-permute-done, bf16[1,1,2,128,128,128]{5,4,3,2,1,0:T(8,128)(2,1)} %param.7, pred[]{:T(512)} %bitcast), kind=kLoop, calls=%fused_computation.16 | loop fusion | flops 2097152 | bytes 12582913 | tf_op jit(solution)/shard_map/jit(_where)/select_n | solution.py:82
  79.5 0.8 fusion.97
  80.3 1.3 fusion.47
  81.6 1.3 fusion.50
  82.9 1.3 fusion.53
  84.2 1.6 broadcast.22
  85.8 2.1 %fusion.86 = f32[512,1024]{1,0:T(8,128)} fusion(f32[512,1024]{1,0:T(8,128)} %broadcast.22, s32[]{:T(128)S(6)} %select_n.123, f32[128,1024]{1,0:T(8,128)S(1)} %fusion.53, f32[128,1024]{1,0:T(8,128)S(1)} %fusion.50, f32[128,1024]{1,0:T(8,128)S(1)} %fusion.47, bf16[128,1024]{1,0:T(8,128)(2,1)S(1)} %bitcast_select_fusion.1, ...), kind=kOutput, calls=%fused_computation.53 | convolution fusion | flops 1078460416 | bytes 3473416 | tf_op jit(solution)/shard_map/dot_general | solution.py:49
  88.0 58.0 %all-reduce.1 = bf16[512,1024]{1,0:T(8,128)(2,1)S(1)} all-reduce(f32[512,1024]{1,0:T(8,128)} %fusion.86), channel_id=1, replica_groups=mesh['ia'=4,'ja'=4,'ka'=2] {'ja','ka'}, use_global_device_ids=true, to_apply=%region_0.1 | all-reduce | flops 524288 | bytes 3145728 | tf_op jit(solution)/shard_map/psum | solution.py:92
  146.0 1.3 convolution_convert_fusion
  147.3 1.0 copy-done.3
  148.3 2.6 %fusion.35 = f32[128,1024]{1,0:T(8,128)S(1)} fusion(bf16[128,128,128]{2,1,0:T(8,128)(2,1)} %copy-done.1, bf16[32,1024]{1,0:T(8,128)(2,1)S(1)} %get-tuple-element.8, bf16[128,1024]{1,0:T(8,128)(2,1)S(1)} %bitcast_select_fusion.1), kind=kOutput, calls=%fused_computation.36 | convolution fusion | flops 1090519040 | bytes 5046272 | tf_op jit(solution)/shard_map/dot_general | solution.py:49
  151.0 1.3 fusion.38
  152.3 1.3 fusion.41
  153.6 1.6 broadcast_in_dim.9
  155.2 2.3 %fusion.77 = f32[1,512,1024]{2,1,0:T(8,128)} fusion(f32[1,512,1024]{2,1,0:T(8,128)} %broadcast_in_dim.9, s32[]{:T(128)S(6)} %select_n.116, f32[128,1024]{1,0:T(8,128)S(1)} %fusion.41, f32[128,1024]{1,0:T(8,128)S(1)} %fusion.38, f32[128,1024]{1,0:T(8,128)S(1)} %fusion.35, bf16[128,128,128]{2,1,0:T(8,128)(2,1)S(1)} %copy-done.2, ...), kind=kOutput, calls=%fused_computation.50 | convolution fusion | flops 1091043328 | bytes 6619144 | tf_op jit(solution)/shard_map/dot_general | solution.py:49
  157.5 0.0 reduce-scatter.2.cloned.1.call-update
  157.6 1.6 dynamic-slice_bitcast_fusion.1
  159.1 32.4 %reduce-scatter.2.cloned.1.call-done = f32[1,64,1024]{2,1,0:T(8,128)} async-done(((f32[1,512,1024]{2,1,0:T(8,128)}), f32[1,64,1024]{2,1,0:T(8,128)}) %reduce-scatter.2.cloned.1.call-update) | async-done | bytes 262160 | tf_op jit(solution)/shard_map/reduce_scatter | solution.py:105
  191.5 2.8 %fusion.89 = bf16[1,64,1024]{2,1,0:T(8,128)(2,1)} fusion(bf16[1024,1024]{1,0:T(8,128)(2,1)} %param.13, f32[1,64,1024]{2,1,0:T(8,128)} %reduce-scatter.2.cloned.1.call-done), kind=kOutput, calls=%fused_computation.55 | convolution fusion | flops 134348800 | bytes 2490368 | tf_op jit(solution)/shard_map/dot_general | solution.py:108
  (30 shorter events, 0.2 us)
Async XLA Ops:
  7.2 138.9 %copy-start = (bf16[1024,1024]{1,0:T(8,128)(2,1)S(1)}, bf16[1024,1024]{1,0:T(8,128)(2,1)}, u32[]{:S(2)}) copy-start(bf16[1024,1024]{1,0:T(8,128)(2,1)} %param.12) | copy-start | bytes 6291460
  7.2 5.4 %copy-start.4 = (bf16[1,64,1024]{2,1,0:T(8,128)(2,1)S(1)}, bf16[1,64,1024]{2,1,0:T(8,128)(2,1)}, u32[]{:S(2)}) copy-start(bf16[1,64,1024]{2,1,0:T(8,128)(2,1)} %param.10) | copy-start | bytes 393220
  7.2 10.2 %copy-start.5 = (s32[3,1,1,2]{0,3,2,1:T(2,128)S(1)}, s32[3,1,1,2]{0,3,2,1:T(2,128)}, u32[]{:S(2)}) copy-start(s32[3,1,1,2]{0,3,2,1:T(2,128)} %param.8) | copy-start | bytes 76
  7.2 10.8 %copy-start.6 = (s32[1,1,2]{2,1,0:T(1,128)S(1)}, s32[1,1,2]{2,1,0:T(1,128)}, u32[]{:S(2)}) copy-start(s32[1,1,2]{2,1,0:T(1,128)} %param.9) | copy-start | bytes 28
  7.2 64.7 %all-gather.2.cloned.1.call-start = ((), (), s32[]{:S(2)}) async-start(), calls=%async_computation.1 | async-start | bytes 1114112 | tf_op jit(solution)/shard_map/all_gather | solution.py:75
  12.1 63.4 %collective-permute-start = (bf16[128,128,128]{2,1,0:T(8,128)(2,1)}, bf16[128,128,128]{2,1,0:T(8,128)(2,1)}, u32[]{:S(2)}, u32[]{:S(2)}) collective-permute-start(bf16[128,128,128]{2,1,0:T(8,128)(2,1)} %slice_bitcast_fusion), channel_id=1, source_target_pairs={{1,0},{0,1},{3,2},{2,3},{5,4},{4,5},{7,6},{6,7},{9,8},{8,9},{11,10... | collective-permute-start | bytes 12582920 | tf_op jit(solution)/shard_map/ppermute | solution.py:34
  12.6 14.0 %collective-permute-start.1 = (bf16[1,64,1024]{2,1,0:T(8,128)(2,1)S(1)}, bf16[1,64,1024]{2,1,0:T(8,128)(2,1)S(1)}, u32[]{:S(2)}, u32[]{:S(2)}) collective-permute-start(bf16[1,64,1024]{2,1,0:T(8,128)(2,1)S(1)} %copy-done.4), channel_id=1, source_target_pairs={{0,1},{1,8},{8,9},{9,16},{16,17},{17,24},{24,25},{25,0},{2,3},{3,1... | collective-permute-start | bytes 393224 | tf_op jit(solution)/shard_map/ppermute | solution.py:19
  12.6 14.5 %collective-permute-start.2 = (bf16[1,64,1024]{2,1,0:T(8,128)(2,1)S(1)}, bf16[1,64,1024]{2,1,0:T(8,128)(2,1)S(1)}, u32[]{:S(2)}, u32[]{:S(2)}) collective-permute-start(bf16[1,64,1024]{2,1,0:T(8,128)(2,1)S(1)} %copy-done.4), channel_id=1, source_target_pairs={{0,25},{1,0},{8,1},{9,8},{16,9},{17,16},{24,17},{25,24},{2,27},{3,... | collective-permute-start | bytes 393224 | tf_op jit(solution)/shard_map/ppermute | solution.py:24
  17.3 174.2 %reduce-scatter.2.cloned.1.call-start = ((), (), s32[]{:S(2)}) async-start(), calls=%async_computation.2 | async-start | bytes 2359296 | tf_op jit(solution)/shard_map/reduce_scatter | solution.py:105
  20.5 2.2 %collective-permute-start.8 = (bf16[3]{0:T(256)(128)(2,1)S(1)}, bf16[3]{0:T(256)(128)(2,1)S(1)}, u32[]{:S(2)}, u32[]{:S(2)}) collective-permute-start(bf16[3]{0:T(256)(128)(2,1)S(1)} %pad_maximum_fusion), channel_id=1, source_target_pairs={{1,0},{0,1},{3,2},{2,3},{5,4},{4,5},{7,6},{6,7},{9,8},{8,9},{11,10... | collective-permute-start | bytes 26 | tf_op jit(solution)/shard_map/ppermute | solution.py:34
  26.6 7.5 %collective-permute-start.3 = (bf16[1,64,1024]{2,1,0:T(8,128)(2,1)S(1)}, bf16[1,64,1024]{2,1,0:T(8,128)(2,1)S(1)}, u32[]{:S(2)}, u32[]{:S(2)}) collective-permute-start(bf16[1,64,1024]{2,1,0:T(8,128)(2,1)S(1)} %collective-permute-done.1), channel_id=1, source_target_pairs={{0,1},{1,8},{8,9},{9,16},{16,17},{17,24},{24,25},{25,0},{2,3},{3,1... | collective-permute-start | bytes 393224 | tf_op jit(solution)/shard_map/ppermute | solution.py:19
  27.1 6.9 %collective-permute-start.4 = (bf16[1,64,1024]{2,1,0:T(8,128)(2,1)S(1)}, bf16[1,64,1024]{2,1,0:T(8,128)(2,1)S(1)}, u32[]{:S(2)}, u32[]{:S(2)}) collective-permute-start(bf16[1,64,1024]{2,1,0:T(8,128)(2,1)S(1)} %collective-permute-done.2), channel_id=1, source_target_pairs={{0,25},{1,0},{8,1},{9,8},{16,9},{17,16},{24,17},{25,24},{2,27},{3,... | collective-permute-start | bytes 393224 | tf_op jit(solution)/shard_map/ppermute | solution.py:24
  34.0 6.8 %collective-permute-start.5 = (bf16[1,64,1024]{2,1,0:T(8,128)(2,1)S(1)}, bf16[1,64,1024]{2,1,0:T(8,128)(2,1)S(1)}, u32[]{:S(2)}, u32[]{:S(2)}) collective-permute-start(bf16[1,64,1024]{2,1,0:T(8,128)(2,1)S(1)} %collective-permute-done.3), channel_id=1, source_target_pairs={{0,1},{1,8},{8,9},{9,16},{16,17},{17,24},{24,25},{25,0},{2,3},{3,1... | collective-permute-start | bytes 393224 | tf_op jit(solution)/shard_map/ppermute | solution.py:19
  34.0 6.8 %collective-permute-start.6 = (bf16[1,64,1024]{2,1,0:T(8,128)(2,1)S(1)}, bf16[1,64,1024]{2,1,0:T(8,128)(2,1)S(1)}, u32[]{:S(2)}, u32[]{:S(2)}) collective-permute-start(bf16[1,64,1024]{2,1,0:T(8,128)(2,1)S(1)} %collective-permute-done.4), channel_id=1, source_target_pairs={{0,25},{1,0},{8,1},{9,8},{16,9},{17,16},{24,17},{25,24},{2,27},{3,... | collective-permute-start | bytes 393224 | tf_op jit(solution)/shard_map/ppermute | solution.py:24
  40.8 32.2 %collective-permute-start.7 = (bf16[1,64,1024]{2,1,0:T(8,128)(2,1)S(1)}, bf16[1,64,1024]{2,1,0:T(8,128)(2,1)S(1)}, u32[]{:S(2)}, u32[]{:S(2)}) collective-permute-start(bf16[1,64,1024]{2,1,0:T(8,128)(2,1)S(1)} %collective-permute-done.5), channel_id=1, source_target_pairs={{0,1},{1,8},{8,9},{9,16},{16,17},{17,24},{24,25},{25,0},{2,3},{3,1... | collective-permute-start | bytes 393224 | tf_op jit(solution)/shard_map/ppermute | solution.py:19
  72.9 1.6 collective-permute-start.9
  79.5 2.1 %copy-start.1 = (bf16[128,128,128]{2,1,0:T(8,128)(2,1)}, bf16[128,128,128]{2,1,0:T(8,128)(2,1)S(1)}, u32[]{:S(2)}) copy-start(bf16[128,128,128]{2,1,0:T(8,128)(2,1)S(1)} %bitcast_select_fusion) | copy-start | bytes 12582916
  147.3 1.0 copy-start.3
  148.3 2.7 %copy-start.2 = (bf16[128,128,128]{2,1,0:T(8,128)(2,1)S(1)}, bf16[128,128,128]{2,1,0:T(8,128)(2,1)}, u32[]{:S(2)}) copy-start(bf16[128,128,128]{2,1,0:T(8,128)(2,1)} %copy-done.1) | copy-start | bytes 12582916
Sparse Core Ops, SparseCore 0:
  17.5 54.4 all-gather.1
  157.7 33.7 reduce-scatter.1
